TPU v7x, 32 devices: a whole 2x2x4 slice. The times are simulated.
32 devices in a mesh: seq: 16 (over z, y, x), mdl: 2 (over core).
Axes of the slice: x: 2, y: 2, z: 4, core: 2. Of those that a mesh axis runs over, the one named last changes fastest.
Arguments:
- hidden_in: bfloat16 [32, 4, 2048], P(None, None, 'seq'), may hold values from -25 to 25
- cache_keys: bfloat16 [32, 512, 2048], P(None, 'seq', 'mdl'), may hold values from -250 to 250, as said below
- cache_values: bfloat16 [32, 512, 2048], P(None, 'seq', 'mdl'), may hold values from -6 to 6
- lengths: int32 [32], replicated, may hold values from 1 to 508, as said below
- query_weight: bfloat16 [2048, 2048], P('seq', 'mdl'), may hold values from -0.125 to 0.125
- key_weight: bfloat16 [2048, 2048], P('seq', 'mdl'), may hold values from -0.125 to 0.125
- value_weight: bfloat16 [2048, 2048], P('seq', 'mdl'), may hold values from -0.125 to 0.125
- out_weight: bfloat16 [2048, 2048], P('mdl', 'seq'), may hold values from -0.125 to 0.125
- gate_weight: bfloat16 [2048, 8192], P('seq', 'mdl'), may hold values from -0.125 to 0.125
- up_weight: bfloat16 [2048, 8192], P('seq', 'mdl'), may hold values from -0.125 to 0.125
- down_weight: bfloat16 [8192, 2048], P('mdl', 'seq'), may hold values from -0.0625 to 0.0625
Outputs:
- hidden_out: bfloat16 [32, 4, 2048], P(None, None, 'seq')
- new_cache_keys: bfloat16 [32, 512, 2048], P(None, 'seq', 'mdl')
- new_cache_values: bfloat16 [32, 512, 2048], P(None, 'seq', 'mdl')
Inputs may be any that keep to these rules, and one draw needn't show every extreme that they name: `cache_keys`: keys are stored after their rotary embedding. `lengths`: at least one request has exactly 508 cached positions.
All inputs are finite; a program needn't handle non-finite values.
Results may differ from a plain program's by a relative error of at most 0.012.
The roundings to bfloat16 on the way count: a program that leaves them out, or rounds other values in their place, can miss the bound.
Values may be sent and summed in bfloat16 or wider, within the bound.
A program may use at most 64 MiB of HBM per device.

v0:
```python
import math
import jax
import jax.numpy as jnp
from jax import lax
from jax.sharding import PartitionSpec as P

D = 2048
HEADS = 16
EPS = 1e-05
THETA = 10000.0
NEGATIVE = -1e30


def rotate(vectors, placed_pos):
    head_size = vectors.shape[-1]
    half_dim = head_size // 2
    freqs = THETA ** (-jnp.arange(half_dim, dtype=jnp.float32) * 2.0 / head_size)
    angles = placed_pos.astype(jnp.float32)[..., None, None] * freqs
    cosine = jnp.cos(angles)
    sine = jnp.sin(angles)
    first_half = vectors[..., :half_dim]
    second_half = vectors[..., half_dim:]
    return jnp.concatenate(
        [first_half * cosine - second_half * sine, second_half * cosine + first_half * sine],
        axis=-1,
    )


def normalize(widened, row_sums, square_sums):
    row_mean = row_sums / D
    second_moment = square_sums / D
    inverse = 1.0 / jnp.sqrt(second_moment - row_mean * row_mean + EPS)
    return ((widened - row_mean[..., None]) * inverse[..., None]).astype(jnp.bfloat16)


def body(
    hidden_in,
    cache_keys,
    cache_values,
    lengths,
    query_weight,
    key_weight,
    value_weight,
    out_weight,
    gate_weight,
    up_weight,
    down_weight,
):
    requests, token_count, narrow_width = hidden_in.shape
    slot_count = cache_keys.shape[1]
    local_width = cache_keys.shape[2]
    head_size = D // HEADS
    local_heads = local_width // head_size
    score_scale = 1.0 / math.sqrt(head_size)
    shard_index = lax.axis_index("seq")
    slot_ids = shard_index * slot_count + jnp.arange(slot_count, dtype=jnp.int32)
    live_slots = slot_ids[None, :] < lengths[:, None]
    old_keys = cache_keys.reshape(requests, slot_count, local_heads, head_size)
    old_values = cache_values.reshape(requests, slot_count, local_heads, head_size).astype(
        jnp.float32
    )
    positions = lengths[:, None] + jnp.arange(token_count, dtype=jnp.int32)[None, :]
    out_list = []
    key_list = []
    value_list = []
    for token_step in range(1):
        row_block = hidden_in
        block_rows = row_block.shape[1]
        widened = row_block.astype(jnp.float32)
        row_sums, square_sums = lax.psum(
            (jnp.sum(widened, axis=-1), jnp.sum(widened * widened, axis=-1)), "seq"
        )
        normed = normalize(widened, row_sums, square_sums)
        query_part = jnp.einsum(
            "rnc,cm->rnm", normed, query_weight, preferred_element_type=jnp.float32
        )
        key_part = jnp.einsum("rnc,cm->rnm", normed, key_weight, preferred_element_type=jnp.float32)
        value_part = jnp.einsum(
            "rnc,cm->rnm", normed, value_weight, preferred_element_type=jnp.float32
        )
        queries, keys_full, values_full = lax.psum((query_part, key_part, value_part), "seq")
        placed_pos = positions[:, token_step : token_step + block_rows]
        queries = rotate(
            queries.reshape(requests, block_rows, local_heads, head_size), placed_pos
        ).astype(jnp.bfloat16)
        new_key = rotate(
            keys_full.reshape(requests, block_rows, local_heads, head_size), placed_pos
        ).astype(jnp.bfloat16)
        new_value = values_full.reshape(requests, block_rows, local_heads, head_size).astype(
            jnp.bfloat16
        )
        keys_new = jnp.concatenate(key_list + [new_key], axis=1)
        values_new = jnp.concatenate(value_list + [new_value], axis=1)
        old_scores = (
            jnp.einsum("rnhd,rjhd->rnhj", queries, old_keys, preferred_element_type=jnp.float32)
            * score_scale
        )
        old_scores = jnp.where(live_slots[:, None, None, :], old_scores, NEGATIVE)
        top_old = jnp.max(old_scores, axis=-1)
        weights_old = jnp.where(
            live_slots[:, None, None, :], jnp.exp(old_scores - top_old[..., None]), 0.0
        )
        total_old = jnp.sum(weights_old, axis=-1)
        summed_old = jnp.einsum(
            "rnhj,rjhd->rnhd", weights_old, old_values, precision=lax.Precision.HIGHEST
        )
        top_cache = lax.pmax(top_old, "seq")
        factor_old = jnp.exp(top_old - top_cache)
        total_cache, summed_cache = lax.psum(
            (total_old * factor_old, summed_old * factor_old[..., None]), "seq"
        )
        new_scores = (
            jnp.einsum("rnhd,rshd->rnhs", queries, keys_new, preferred_element_type=jnp.float32)
            * score_scale
        )
        key_index = jnp.arange(keys_new.shape[1], dtype=jnp.int32)
        query_index = token_step + jnp.arange(block_rows, dtype=jnp.int32)
        allowed = key_index[None, :] <= query_index[:, None]
        new_scores = jnp.where(allowed[None, :, None, :], new_scores, NEGATIVE)
        top_new = jnp.max(new_scores, axis=-1)
        weights_new = jnp.exp(new_scores - top_new[..., None])
        total_new = jnp.sum(weights_new, axis=-1)
        summed_new = jnp.einsum(
            "rnhs,rshd->rnhd",
            weights_new,
            values_new.astype(jnp.float32),
            precision=lax.Precision.HIGHEST,
        )
        top_score = jnp.maximum(top_cache, top_new)
        factor_cache = jnp.exp(top_cache - top_score)
        factor_new = jnp.exp(top_new - top_score)
        running = total_cache * factor_cache + total_new * factor_new
        combined = summed_cache * factor_cache[..., None] + summed_new * factor_new[..., None]
        attended = (
            (combined / running[..., None])
            .astype(jnp.bfloat16)
            .reshape(requests, block_rows, local_width)
        )
        attn_part = jnp.einsum(
            "rnm,mc->rnc", attended, out_weight, preferred_element_type=jnp.float32
        )
        mixed = widened + lax.psum(attn_part, "mdl")
        sums_mixed, squares_mixed = lax.psum(
            (jnp.sum(mixed, axis=-1), jnp.sum(mixed * mixed, axis=-1)), "seq"
        )
        normed2 = normalize(mixed, sums_mixed, squares_mixed)
        gate_part = jnp.einsum(
            "rnc,cf->rnf", normed2, gate_weight, preferred_element_type=jnp.float32
        )
        up_part = jnp.einsum("rnc,cf->rnf", normed2, up_weight, preferred_element_type=jnp.float32)
        gate_full, up_full = lax.psum((gate_part, up_part), "seq")
        act_full = (jax.nn.silu(gate_full) * up_full).astype(jnp.bfloat16)
        down_part = jnp.einsum(
            "rnf,fc->rnc", act_full, down_weight, preferred_element_type=jnp.float32
        )
        block_out = (mixed + lax.psum(down_part, "mdl")).astype(jnp.bfloat16)
        block_out, new_key, new_value = (block_out, new_key, new_value)
        out_list.append(block_out)
        key_list.append(new_key)
        value_list.append(new_value)
    hidden_out = jnp.concatenate(out_list, axis=1)
    keys_all = jnp.concatenate(key_list, axis=1)
    values_all = jnp.concatenate(value_list, axis=1)
    slot_hits = slot_ids[None, None, :] == positions[:, :, None]
    one_hot = slot_hits.astype(jnp.bfloat16)
    written = jnp.any(slot_hits, axis=1)[..., None]
    placed_keys = jnp.einsum(
        "rts,rtm->rsm",
        one_hot,
        keys_all.reshape(requests, token_count, local_width),
        preferred_element_type=jnp.float32,
    ).astype(jnp.bfloat16)
    placed_values = jnp.einsum(
        "rts,rtm->rsm",
        one_hot,
        values_all.reshape(requests, token_count, local_width),
        preferred_element_type=jnp.float32,
    ).astype(jnp.bfloat16)
    new_cache_keys = jnp.where(written, placed_keys, cache_keys)
    new_cache_values = jnp.where(written, placed_values, cache_values)
    return (hidden_out, new_cache_keys, new_cache_values)


def solution(mesh):
    placed = (
        P(None, None, "seq"),
        P(None, "seq", "mdl"),
        P(None, "seq", "mdl"),
        P(),
        P("seq", "mdl"),
        P("seq", "mdl"),
        P("seq", "mdl"),
        P("mdl", "seq"),
        P("seq", "mdl"),
        P("seq", "mdl"),
        P("mdl", "seq"),
    )
    return jax.shard_map(
        body,
        mesh=mesh,
        in_specs=placed,
        out_specs=(P(None, None, "seq"), P(None, "seq", "mdl"), P(None, "seq", "mdl")),
        check_vma=False,
    )
```

profile of v0, /device:TPU:0, one launch (start us, length us, event | category | flops | bytes accessed | tf_op | source)
XLA Modules:
  0.0 622.2 jit_solution(543046160231867355)
XLA Ops:
  7.2 1.0 convert_reduce_fusion
  8.2 43.5 %all-reduce.2 = (f32[32,4]{0,1:T(4,128)S(1)}, f32[32,4]{0,1:T(4,128)S(1)}) all-reduce(f32[32,4]{0,1:T(4,128)S(1)} %get-tuple-element.12, f32[32,4]{0,1:T(4,128)S(1)} %get-tuple-element.11), channel_id=1, replica_groups=mesh['seq'=16,'mdl'=2] {'seq'}, use_global_device_ids=true, to_apply=%region_3.0 | all-reduce | flops 256 | bytes 2048 | tf_op jit(solution)/shard_map/psum | solution.py:70
  51.7 1.2 fusion.42
  53.1 1.1 copy.23
  54.7 1.1 copy.26
  56.5 102.0 %all-reduce.12.cloned.1.call-done = f32[32,4,8,128]{3,1,2,0:T(4,128)} async-done(((f32[32,4,8,128]{3,1,2,0:T(4,128)}), f32[32,4,8,128]{3,1,2,0:T(4,128)}) %all-reduce.12.cloned.1.call-update) | async-done | bytes 524304 | tf_op jit(solution)/shard_map/psum | solution.py:81
  158.5 1.7 subtract_convert_fusion
  160.3 4.0 fusion.71
  164.2 75.7 %pmax.7 = f32[32,4,8]{1,2,0:T(8,128)S(1)} all-reduce(f32[32,4,8]{1,2,0:T(8,128)S(1)} %get-tuple-element.40), channel_id=1, replica_groups=mesh['seq'=16,'mdl'=2] {'seq'}, use_global_device_ids=true, to_apply=%region_6.0 | all-reduce | flops 1024 | bytes 8192 | tf_op jit(solution)/shard_map/pmax | solution.py:107
  240.0 1.7 fusion.34
  241.7 0.7 fusion.70
  242.4 3.7 fusion.9
  246.2 1.3 fusion.38
  247.4 82.0 %all-reduce.21 = (bf16[32,4,1024]{2,0,1:T(8,128)(2,1)S(1)}, f32[32,4,8]{1,2,0:T(8,128)S(1)}) all-reduce(f32[32,4,1024]{2,0,1:T(8,128)S(1)} %fusion.38, f32[32,4,8]{1,2,0:T(8,128)} %get-tuple-element.26), channel_id=1, replica_groups=mesh['seq'=16,'mdl'=2] {'seq'}, use_global_device_ids=true, to_apply=%region_10.11 | all-reduce | flops 132096 | bytes 794624 | tf_op jit(solution)/shard_map/psum | solution.py:81
  329.5 27.1 %all-reduce.20.cloned.1.call-done = (f32[32,4,8,128]{3,1,2,0:T(4,128)}, f32[32,4,8,128]{3,1,2,0:T(4,128)}) async-done(((f32[32,4,8,128]{3,1,2,0:T(4,128)}, f32[32,4,8,128]{3,1,2,0:T(4,128)}), (f32[32,4,8,128]{3,1,2,0:T(4,128)}, f32[32,4,8,128]{3,1,2,0:T(4,128)})) %all-reduce.20.cloned.1.call-update) | async-done | bytes 1048592 | tf_op jit(solution)/shard_map/psum | solution.py:109
  356.7 1.7 multiply_subtract_fusion
  358.4 2.1 fusion.72
  361.1 2.1 fusion.26
  363.3 0.8 fusion.36
  364.3 16.7 %all-reduce.14.cloned.1.call-done = f32[32,4,128]{2,0,1:T(8,128)} async-done(((f32[32,4,128]{2,0,1:T(8,128)}), f32[32,4,128]{2,0,1:T(8,128)}) %all-reduce.14.cloned.1.call-update) | async-done | bytes 65552 | tf_op jit(solution)/shard_map/psum | solution.py:142
  381.0 1.0 fusion.67
  382.0 42.0 %all-reduce = (f32[32,4]{0,1:T(4,128)S(1)}, f32[32,4]{0,1:T(4,128)S(1)}) all-reduce(f32[32,4]{0,1:T(4,128)S(1)} %get-tuple-element.10, f32[32,4]{0,1:T(4,128)S(1)} %get-tuple-element.9), channel_id=1, replica_groups=mesh['seq'=16,'mdl'=2] {'seq'}, use_global_device_ids=true, to_apply=%region_18.19 | all-reduce | flops 256 | bytes 2048 | tf_op jit(solution)/shard_map/psum | solution.py:143
  424.0 2.6 fusion.29
  426.6 1.8 fusion.31
  428.6 1.5 copy-done.3
  430.1 3.6 convert_select_fusion
  433.7 159.6 %all-reduce.18.cloned.1.call-done = (f32[32,4,4096]{2,0,1:T(8,128)}, f32[32,4,4096]{2,0,1:T(8,128)}) async-done(((f32[32,4,4096]{2,0,1:T(8,128)}, f32[32,4,4096]{2,0,1:T(8,128)}), (f32[32,4,4096]{2,0,1:T(8,128)}, f32[32,4,4096]{2,0,1:T(8,128)})) %all-reduce.18.cloned.1.call-update) | async-done | bytes 4194320 | tf_op jit(solution)/shard_map/psum | solution.py:151
  593.3 4.0 fusion.27
  597.3 3.5 convert_select_fusion.1
  600.8 13.3 %all-reduce.16.cloned.1.call-done = f32[32,4,128]{2,0,1:T(8,128)} async-done(((f32[32,4,128]{2,0,1:T(8,128)}), f32[32,4,128]{2,0,1:T(8,128)}) %all-reduce.16.cloned.1.call-update) | async-done | bytes 65552 | tf_op jit(solution)/shard_map/psum | solution.py:156
  614.2 0.9 add_convert_fusion.1
  615.0 0.6 copy.31
  (66 shorter events, 2.4 us)
Async XLA Ops:
  7.2 416.8 %copy-start = (bf16[128,4096]{1,0:T(8,128)(2,1)S(1)}, bf16[128,4096]{1,0:T(8,128)(2,1)}, u32[]{:S(2)}) copy-start(bf16[128,4096]{1,0:T(8,128)(2,1)} %param.20) | copy-start | bytes 3145732
  7.2 47.1 %copy-start.1 = (bf16[32,4,128]{2,1,0:T(4,128)(2,1)S(1)}, bf16[32,4,128]{2,1,0:T(4,128)(2,1)}, u32[]{:S(2)}) copy-start(bf16[32,4,128]{2,1,0:T(4,128)(2,1)} %param.11) | copy-start | bytes 98308
  7.2 47.1 %copy-start.13 = (bf16[128,1024]{1,0:T(8,128)(2,1)S(1)}, bf16[128,1024]{1,0:T(8,128)(2,1)}, u32[]{:S(2)}) copy-start(bf16[128,1024]{1,0:T(8,128)(2,1)} %param.16) | copy-start | bytes 786436
  7.2 151.3 %all-reduce.12.cloned.1.call-start = ((), (), s32[]{:S(2)}) async-start(), calls=%async_computation | async-start | bytes 1048576 | tf_op jit(solution)/shard_map/psum | solution.py:81
  53.1 2.8 copy-start.18
  54.2 302.4 %all-reduce.20.cloned.1.call-start = ((), (), s32[]{:S(2)}) async-start(), calls=%async_computation.4 | async-start | bytes 2097152 | tf_op jit(solution)/shard_map/psum | solution.py:109
  56.5 107.7 %copy-start.9 = (f32[32,4,64]{2,1,0:T(4,128)}, f32[32,4,64]{2,1,0:T(4,128)S(1)}, u32[]{:S(2)}) copy-start(f32[32,4,64]{2,1,0:T(4,128)S(1)} %get-tuple-element.32) | copy-start | bytes 98308
  56.5 107.7 %copy-start.11 = (f32[32,4,64]{2,1,0:T(4,128)}, f32[32,4,64]{2,1,0:T(4,128)S(1)}, u32[]{:S(2)}) copy-start(f32[32,4,64]{2,1,0:T(4,128)S(1)} %get-tuple-element.33) | copy-start | bytes 98308
  160.2 4.0 copy-start.15
  160.2 4.0 copy-start.17
  160.3 82.1 %copy-start.2 = (bf16[32,32,1024]{2,1,0:T(8,128)(2,1)S(1)}, bf16[32,32,1024]{2,1,0:T(8,128)(2,1)}, u32[]{:S(2)}) copy-start(bf16[32,32,1024]{2,1,0:T(8,128)(2,1)} %param.13) | copy-start | bytes 6291460
  246.1 110.6 %copy-start.10 = (f32[32,4,64]{2,1,0:T(4,128)S(1)}, f32[32,4,64]{2,1,0:T(4,128)}, u32[]{:S(2)}) copy-start(f32[32,4,64]{2,1,0:T(4,128)} %copy-done.9) | copy-start | bytes 98308
  246.1 110.6 %copy-start.12 = (f32[32,4,64]{2,1,0:T(4,128)S(1)}, f32[32,4,64]{2,1,0:T(4,128)}, u32[]{:S(2)}) copy-start(f32[32,4,64]{2,1,0:T(4,128)} %copy-done.11) | copy-start | bytes 98308
  246.1 112.3 %copy-start.16 = (bf16[32,4,8,64]{3,1,2,0:T(4,128)(2,1)S(1)}, bf16[32,4,8,64]{3,1,2,0:T(4,128)(2,1)}, u32[]{:S(2)}) copy-start(bf16[32,4,8,64]{3,1,2,0:T(4,128)(2,1)} %copy-done.15) | copy-start | bytes 393220
  246.1 134.9 %all-reduce.14.cloned.1.call-start = ((), (), s32[]{:S(2)}) async-start(), calls=%async_computation.1 | async-start | bytes 131072 | tf_op jit(solution)/shard_map/psum | solution.py:142
  329.5 33.6 %copy-start.8 = (bf16[32,4,1024]{2,0,1:T(8,128)(2,1)}, bf16[32,4,1024]{2,0,1:T(8,128)(2,1)S(1)}, u32[]{:S(2)}) copy-start(bf16[32,4,1024]{2,0,1:T(8,128)(2,1)S(1)} %get-tuple-element.15) | copy-start | bytes 786436
  358.4 4.8 copy-start.7
  358.4 2.7 copy-start.19
  361.1 2.3 copy-start.14
  363.3 63.3 %copy-start.6 = (bf16[128,4096]{1,0:T(8,128)(2,1)S(1)}, bf16[128,4096]{1,0:T(8,128)(2,1)}, u32[]{:S(2)}) copy-start(bf16[128,4096]{1,0:T(8,128)(2,1)} %param.19) | copy-start | bytes 3145732
  364.2 229.1 %all-reduce.18.cloned.1.call-start = ((), (), s32[]{:S(2)}) async-start(), calls=%async_computation.3 | async-start | bytes 8388608 | tf_op jit(solution)/shard_map/psum | solution.py:151
  381.0 45.7 %copy-start.5 = (f32[32,4,128]{2,0,1:T(8,128)S(1)}, f32[32,4,128]{2,0,1:T(8,128)}, u32[]{:S(2)}) copy-start(f32[32,4,128]{2,0,1:T(8,128)} %all-reduce.14.cloned.1.call-done) | copy-start | bytes 196612
  428.4 1.7 copy-start.3
  428.5 185.7 %all-reduce.16.cloned.1.call-start = ((), (), s32[]{:S(2)}) async-start(), calls=%async_computation.2 | async-start | bytes 131072 | tf_op jit(solution)/shard_map/psum | solution.py:156
  593.3 4.0 copy-start.4
Sparse Core Ops, SparseCore 0:
  54.3 104.1 all-reduce.11
  246.2 110.4 all-reduce.19
  364.3 16.5 all-reduce.13
  428.6 164.7 all-reduce.17
  597.4 16.6 all-reduce.15
where the time goes:
time: 623 us; the launch traced here: 622 us
  waiting for transfers between devices  319 us (51%)
  blocking collectives  243 us (39%)
  matrix products  31 us (5%)
  between operations  14.1 us (2%)
  other arithmetic  9.96 us (2%)
    psum x1, waiting for transfers between devices, body(): gate_full, up_full = lax.psum((gate_part, up_part), 'seq')  160 us
    psum x1, waiting for transfers between devices, body(): lax.psum((query_part, key_part, value_part), 'seq')  102 us
    psum x1, blocking collectives, body(): lax.psum((query_part, key_part, value_part), 'seq')  82 us
    pmax x1, blocking collectives, body(): top_cache = lax.pmax(top_old, 'seq')  75.7 us
    psum x1, blocking collectives, body(): lax.psum((jnp.sum(widened, axis=-1), jnp.sum(widened * widened, axis=-1))...  43.5 us
    psum x1, blocking collectives, body(): lax.psum((jnp.sum(mixed, axis=-1), jnp.sum(mixed * mixed, axis=-1)), 'seq')  42 us
    psum x1, waiting for transfers between devices, body(): lax.psum((total_old * factor_old, summed_old * factor_old[..., None]), 's...  27.1 us
    psum x1, waiting for transfers between devices, body(): mixed = widened + lax.psum(attn_part, 'mdl')  16.7 us
  transfers between devices with their start and end apart: 5, of which 5 were waited for; matrix products, arithmetic and copies ran while one was open for 2% of the time, Pallas kernels for 0%

commit v1 on v0

--- a/solution.py
+++ b/solution.py
@@ -1,3 +1,4 @@
+import functools
 import math
 import jax
 import jax.numpy as jnp
@@ -9,6 +10,13 @@
 EPS = 1e-05
 THETA = 10000.0
 NEGATIVE = -1e30
+
+
+def _perform_targets(field_in, chip_axis):
+    return lax.all_gather(field_in, axis_name=chip_axis).sum(axis=0)
+
+
+pair_group_over_axis = functools.partial(_perform_targets, chip_axis="mdl")
 
 
 def rotate(vectors, placed_pos):
@@ -153,7 +161,7 @@
         down_part = jnp.einsum(
             "rnf,fc->rnc", act_full, down_weight, preferred_element_type=jnp.float32
         )
-        block_out = (mixed + lax.psum(down_part, "mdl")).astype(jnp.bfloat16)
+        block_out = (mixed + pair_group_over_axis(down_part)).astype(jnp.bfloat16)
         block_out, new_key, new_value = (block_out, new_key, new_value)
         out_list.append(block_out)
         key_list.append(new_key)

time: 623 us -> 606 us (0.973)
  waiting for transfers between devices: 319 us -> 303 us
    psum x1 -> x0, waiting for transfers between devices: 13.3 us -> none  [body(): block_out = (mixed + lax.psum(down_part, 'mdl')).astype(jnp.bfloat16)]
  transfers between devices with their start and end apart: 5 -> 4, of which waited for: 5 -> 4; matrix products, arithmetic and copies ran while one was open for 2% -> 2% of each run, Pallas kernels for 0% -> 0%
where the time goes in v1:
time: 606 us; the launch traced here: 605 us
  waiting for transfers between devices  303 us (50%)
  blocking collectives  245 us (40%)
  matrix products  29.2 us (5%)
  between operations  14.1 us (2%)
  other arithmetic  9.12 us (2%)
    psum x1, waiting for transfers between devices, body(): gate_full, up_full = lax.psum((gate_part, up_part), 'seq')  157 us
    psum x1, waiting for transfers between devices, body(): lax.psum((query_part, key_part, value_part), 'seq')  102 us
    psum x1, blocking collectives, body(): lax.psum((query_part, key_part, value_part), 'seq')  82 us
    pmax x1, blocking collectives, body(): top_cache = lax.pmax(top_old, 'seq')  75.7 us
    psum x1, blocking collectives, body(): lax.psum((jnp.sum(widened, axis=-1), jnp.sum(widened * widened, axis=-1))...  43.5 us
    psum x1, blocking collectives, body(): lax.psum((jnp.sum(mixed, axis=-1), jnp.sum(mixed * mixed, axis=-1)), 'seq')  42 us
    psum x1, waiting for transfers between devices, body(): lax.psum((total_old * factor_old, summed_old * factor_old[..., None]), 's...  27 us
    psum x1, waiting for transfers between devices, body(): mixed = widened + lax.psum(attn_part, 'mdl')  16.7 us
  transfers between devices with their start and end apart: 4, of which 4 were waited for; matrix products, arithmetic and copies ran while one was open for 2% of the time, Pallas kernels for 0%

profile of v1, /device:TPU:0, one launch (start us, length us, event | category | flops | bytes accessed | tf_op | source)
XLA Modules:
  0.0 605.3 jit_solution(7110718772699935229)
XLA Ops:
  7.2 1.0 convert_reduce_fusion
  8.2 43.5 %all-reduce.2 = (f32[32,4]{0,1:T(4,128)S(1)}, f32[32,4]{0,1:T(4,128)S(1)}) all-reduce(f32[32,4]{0,1:T(4,128)S(1)} %get-tuple-element.12, f32[32,4]{0,1:T(4,128)S(1)} %get-tuple-element.11), channel_id=1, replica_groups=mesh['seq'=16,'mdl'=2] {'seq'}, use_global_device_ids=true, to_apply=%region_3.0 | all-reduce | flops 256 | bytes 2048 | tf_op jit(solution)/shard_map/psum | solution.py:78
  51.7 1.2 fusion.42
  53.1 1.1 copy.23
  54.7 1.1 copy.26
  56.0 0.5 multiply_cosine_fusion
  56.5 102.0 %all-reduce.11.cloned.1.call-done = f32[32,4,8,128]{3,1,2,0:T(4,128)} async-done(((f32[32,4,8,128]{3,1,2,0:T(4,128)}), f32[32,4,8,128]{3,1,2,0:T(4,128)}) %all-reduce.11.cloned.1.call-update) | async-done | bytes 524304 | tf_op jit(solution)/shard_map/psum | solution.py:89
  158.5 1.7 subtract_convert_fusion
  160.3 4.0 fusion.71
  164.2 75.7 %pmax.7 = f32[32,4,8]{1,2,0:T(8,128)S(1)} all-reduce(f32[32,4,8]{1,2,0:T(8,128)S(1)} %get-tuple-element.40), channel_id=1, replica_groups=mesh['seq'=16,'mdl'=2] {'seq'}, use_global_device_ids=true, to_apply=%region_6.0 | all-reduce | flops 1024 | bytes 8192 | tf_op jit(solution)/shard_map/pmax | solution.py:115
  240.0 1.7 fusion.34
  241.7 0.7 fusion.70
  242.4 3.7 fusion.9
  246.2 1.3 fusion.38
  247.4 82.0 %all-reduce.18 = (bf16[32,4,1024]{2,0,1:T(8,128)(2,1)S(1)}, f32[32,4,8]{1,2,0:T(8,128)S(1)}) all-reduce(f32[32,4,1024]{2,0,1:T(8,128)S(1)} %fusion.38, f32[32,4,8]{1,2,0:T(8,128)} %get-tuple-element.26), channel_id=1, replica_groups=mesh['seq'=16,'mdl'=2] {'seq'}, use_global_device_ids=true, to_apply=%region_10.11 | all-reduce | flops 132096 | bytes 794624 | tf_op jit(solution)/shard_map/psum | solution.py:89
  329.5 27.0 %all-reduce.17.cloned.1.call-done = (f32[32,4,8,128]{3,1,2,0:T(4,128)}, f32[32,4,8,128]{3,1,2,0:T(4,128)}) async-done(((f32[32,4,8,128]{3,1,2,0:T(4,128)}, f32[32,4,8,128]{3,1,2,0:T(4,128)}), (f32[32,4,8,128]{3,1,2,0:T(4,128)}, f32[32,4,8,128]{3,1,2,0:T(4,128)})) %all-reduce.17.cloned.1.call-update) | async-done | bytes 1048592 | tf_op jit(solution)/shard_map/psum | solution.py:117
  356.6 1.7 multiply_subtract_fusion
  358.3 2.1 fusion.72
  361.0 2.1 fusion.26
  363.2 0.8 fusion.36
  364.1 16.7 %all-reduce.13.cloned.1.call-done = f32[32,4,128]{2,0,1:T(8,128)} async-done(((f32[32,4,128]{2,0,1:T(8,128)}), f32[32,4,128]{2,0,1:T(8,128)}) %all-reduce.13.cloned.1.call-update) | async-done | bytes 65552 | tf_op jit(solution)/shard_map/psum | solution.py:150
  380.9 1.0 fusion.67
  381.9 42.0 %all-reduce = (f32[32,4]{0,1:T(4,128)S(1)}, f32[32,4]{0,1:T(4,128)S(1)}) all-reduce(f32[32,4]{0,1:T(4,128)S(1)} %get-tuple-element.10, f32[32,4]{0,1:T(4,128)S(1)} %get-tuple-element.9), channel_id=1, replica_groups=mesh['seq'=16,'mdl'=2] {'seq'}, use_global_device_ids=true, to_apply=%region_18.19 | all-reduce | flops 256 | bytes 2048 | tf_op jit(solution)/shard_map/psum | solution.py:151
  423.9 2.7 fusion.31
  426.6 1.8 fusion.29
  428.5 1.5 copy-done.3
  430.1 3.8 convert_select_fusion
  433.8 2.6 convert_select_fusion.1
  436.5 156.9 %all-reduce.15.cloned.1.call-done = (f32[32,4,4096]{2,0,1:T(8,128)}, f32[32,4,4096]{2,0,1:T(8,128)}) async-done(((f32[32,4,4096]{2,0,1:T(8,128)}, f32[32,4,4096]{2,0,1:T(8,128)}), (f32[32,4,4096]{2,0,1:T(8,128)}, f32[32,4,4096]{2,0,1:T(8,128)})) %all-reduce.15.cloned.1.call-update) | async-done | bytes 4194320 | tf_op jit(solution)/shard_map/psum | solution.py:159
  593.3 2.9 fusion.27
  596.2 1.9 all-gather
  598.2 0.6 copy.31
  (69 shorter events, 1.8 us)
Async XLA Ops:
  7.2 416.7 %copy-start = (bf16[128,4096]{1,0:T(8,128)(2,1)S(1)}, bf16[128,4096]{1,0:T(8,128)(2,1)}, u32[]{:S(2)}) copy-start(bf16[128,4096]{1,0:T(8,128)(2,1)} %param.19) | copy-start | bytes 3145732
  7.2 47.1 %copy-start.1 = (bf16[32,4,128]{2,1,0:T(4,128)(2,1)S(1)}, bf16[32,4,128]{2,1,0:T(4,128)(2,1)}, u32[]{:S(2)}) copy-start(bf16[32,4,128]{2,1,0:T(4,128)(2,1)} %param.11) | copy-start | bytes 98308
  7.2 47.1 %copy-start.14 = (bf16[128,1024]{1,0:T(8,128)(2,1)S(1)}, bf16[128,1024]{1,0:T(8,128)(2,1)}, u32[]{:S(2)}) copy-start(bf16[128,1024]{1,0:T(8,128)(2,1)} %param.16) | copy-start | bytes 786436
  7.2 151.3 %all-reduce.11.cloned.1.call-start = ((), (), s32[]{:S(2)}) async-start(), calls=%async_computation | async-start | bytes 1048576 | tf_op jit(solution)/shard_map/psum | solution.py:89
  53.1 2.8 copy-start.19
  54.2 302.3 %all-reduce.17.cloned.1.call-start = ((), (), s32[]{:S(2)}) async-start(), calls=%async_computation.3 | async-start | bytes 2097152 | tf_op jit(solution)/shard_map/psum | solution.py:117
  56.5 107.7 %copy-start.10 = (f32[32,4,64]{2,1,0:T(4,128)}, f32[32,4,64]{2,1,0:T(4,128)S(1)}, u32[]{:S(2)}) copy-start(f32[32,4,64]{2,1,0:T(4,128)S(1)} %get-tuple-element.32) | copy-start | bytes 98308
  56.5 107.7 %copy-start.12 = (f32[32,4,64]{2,1,0:T(4,128)}, f32[32,4,64]{2,1,0:T(4,128)S(1)}, u32[]{:S(2)}) copy-start(f32[32,4,64]{2,1,0:T(4,128)S(1)} %get-tuple-element.33) | copy-start | bytes 98308
  160.2 4.0 copy-start.16
  160.2 4.0 copy-start.18
  160.3 82.1 %copy-start.2 = (bf16[32,32,1024]{2,1,0:T(8,128)(2,1)S(1)}, bf16[32,32,1024]{2,1,0:T(8,128)(2,1)}, u32[]{:S(2)}) copy-start(bf16[32,32,1024]{2,1,0:T(8,128)(2,1)} %param.13) | copy-start | bytes 6291460
  246.1 110.5 %copy-start.11 = (f32[32,4,64]{2,1,0:T(4,128)S(1)}, f32[32,4,64]{2,1,0:T(4,128)}, u32[]{:S(2)}) copy-start(f32[32,4,64]{2,1,0:T(4,128)} %copy-done.10) | copy-start | bytes 98308
  246.1 110.5 %copy-start.13 = (f32[32,4,64]{2,1,0:T(4,128)S(1)}, f32[32,4,64]{2,1,0:T(4,128)}, u32[]{:S(2)}) copy-start(f32[32,4,64]{2,1,0:T(4,128)} %copy-done.12) | copy-start | bytes 98308
  246.1 112.2 %copy-start.17 = (bf16[32,4,8,64]{3,1,2,0:T(4,128)(2,1)S(1)}, bf16[32,4,8,64]{3,1,2,0:T(4,128)(2,1)}, u32[]{:S(2)}) copy-start(bf16[32,4,8,64]{3,1,2,0:T(4,128)(2,1)} %copy-done.16) | copy-start | bytes 393220
  246.1 134.8 %all-reduce.13.cloned.1.call-start = ((), (), s32[]{:S(2)}) async-start(), calls=%async_computation.1 | async-start | bytes 131072 | tf_op jit(solution)/shard_map/psum | solution.py:150
  329.5 33.5 %copy-start.9 = (bf16[32,4,1024]{2,0,1:T(8,128)(2,1)}, bf16[32,4,1024]{2,0,1:T(8,128)(2,1)S(1)}, u32[]{:S(2)}) copy-start(bf16[32,4,1024]{2,0,1:T(8,128)(2,1)S(1)} %get-tuple-element.15) | copy-start | bytes 786436
  358.3 2.7 copy-start.7
  358.3 2.7 copy-start.21
  360.9 2.2 copy-start.15
  363.2 63.4 %copy-start.6 = (bf16[128,4096]{1,0:T(8,128)(2,1)S(1)}, bf16[128,4096]{1,0:T(8,128)(2,1)}, u32[]{:S(2)}) copy-start(bf16[128,4096]{1,0:T(8,128)(2,1)} %param.20) | copy-start | bytes 3145732
  364.1 229.2 %all-reduce.15.cloned.1.call-start = ((), (), s32[]{:S(2)}) async-start(), calls=%async_computation.2 | async-start | bytes 8388608 | tf_op jit(solution)/shard_map/psum | solution.py:159
  380.9 45.7 %copy-start.5 = (f32[32,4,128]{2,0,1:T(8,128)S(1)}, f32[32,4,128]{2,0,1:T(8,128)}, u32[]{:S(2)}) copy-start(f32[32,4,128]{2,0,1:T(8,128)} %all-reduce.13.cloned.1.call-done) | copy-start | bytes 196612
  428.4 1.7 copy-start.3
  430.1 3.8 copy-start.4
  430.1 3.8 copy-start.8
  433.8 159.5 %copy-start.20 = (bf16[4096,128]{1,0:T(8,128)(2,1)S(1)}, bf16[4096,128]{1,0:T(8,128)(2,1)}, u32[]{:S(2)}) copy-start(bf16[4096,128]{1,0:T(8,128)(2,1)} %param.21) | copy-start | bytes 3145732
Sparse Core Ops, SparseCore 0:
  54.3 104.1 all-reduce.10
  246.2 110.2 all-reduce.16
  364.2 16.6 all-reduce.12
  428.5 164.7 all-reduce.14
